TPU v7x, 256 devices: a whole 4x4x8 slice. The times are simulated.
256 devices in a mesh: head: 16 (over y, x_lo, core), ctx: 16 (over x_hi, z).
Axes of the slice: x: 4 (x_hi: 2, x_lo: 2; x = x_hi * 2 + x_lo), y: 4, z: 8, core: 2. Of those that a mesh axis runs over, the one named last changes fastest.
Arguments:
- queries: bfloat16 [65536, 2048], P(('ctx', 'head')), may hold values from -6 to 6
- keys: bfloat16 [65536, 2048], P(('ctx', 'head')), may hold values from -6 to 6
- values: bfloat16 [65536, 2048], P(('ctx', 'head')), may hold values from -24 to 24
- picks: int32 [128, 2], replicated, may hold values from 0 to 127, as said below
Outputs:
- attended: bfloat16 [65536, 2048], P(('ctx', 'head'))
Inputs may be any that keep to these rules, and one draw needn't show every extreme that they name: `picks`: rows 8 * c to 8 * c + 7 are the query blocks held by index c of ctx, and blocks 8 * o to 8 * o + 7 are held by index o. Among the 16 entries of one such group of rows, at most 2 name blocks held by any one index of ctx; one index o, the same for every group, is named exactly 2 times by every group.
All inputs are finite; a program needn't handle non-finite values.
Results may differ from a plain program's by a relative error of at most 0.0039.
Values may be sent and summed in bfloat16 or wider, within the bound.
A program may use at most 128 MiB of HBM per device.

v0:
```python
import math
import jax
import jax.numpy as jnp
from jax import lax
from jax.sharding import PartitionSpec as P

HEADS = 16
HD = 128
BLOCK = 512
RSEL = 2


def block_pair(query_block, key_block, value_block, score_scale):
    scores = (
        jnp.einsum("qhd,khd->hqk", query_block, key_block, preferred_element_type=jnp.float32)
        * score_scale
    )
    row_max = jnp.max(scores, axis=-1)
    exponent = jnp.exp(scores - row_max[..., None])
    row_sum = jnp.sum(exponent, axis=-1)
    weights = exponent.astype(jnp.bfloat16)
    partial_out = jnp.einsum(
        "hqk,khd->qhd", weights, value_block, preferred_element_type=jnp.float32
    )
    return (partial_out, row_max, row_sum)


def route_tables(picks, local_blocks, ctx_count):
    slots = local_blocks * RSEL
    owners = (picks // local_blocks).reshape(ctx_count, slots)
    within = (picks % local_blocks).reshape(ctx_count, slots)
    owner_ids = jnp.arange(ctx_count, dtype=jnp.int32)
    one_hot = (owners[:, :, None] == owner_ids[None, None, :]).astype(jnp.int32)
    running = jnp.cumsum(one_hot, axis=1)
    position = jnp.sum(one_hot * running, axis=-1) - 1
    return (owners, within, position)


def local(queries, keys, values, picks):
    head_count = lax.axis_size("head")
    ctx_count = lax.axis_size("ctx")
    my_index = lax.axis_index("ctx")
    heads_here = HEADS // head_count
    tok_rows = queries.shape[0]
    score_scale = 1.0 / math.sqrt(HD)
    q_split = queries.reshape(tok_rows, HEADS, HD)
    k_split = keys.reshape(tok_rows, HEADS, HD)
    v_split = values.reshape(tok_rows, HEADS, HD)
    q_heads, k_heads, v_heads = (
        lax.all_to_all(q_split, "head", split_axis=1, concat_axis=0, tiled=True),
        lax.all_to_all(k_split, "head", split_axis=1, concat_axis=0, tiled=True),
        lax.all_to_all(v_split, "head", split_axis=1, concat_axis=0, tiled=True),
    )
    local_blocks = q_heads.shape[0] // BLOCK
    q_blocks = q_heads.reshape(local_blocks, BLOCK, heads_here, HD)
    k_blocks = k_heads.reshape(local_blocks, BLOCK, heads_here, HD)
    v_blocks = v_heads.reshape(local_blocks, BLOCK, heads_here, HD)
    capacity = (local_blocks * RSEL + ctx_count - 1) // ctx_count + 1
    slots = local_blocks * RSEL
    owners, within, position = route_tables(picks, local_blocks, ctx_count)
    mine_owner = lax.dynamic_index_in_dim(owners, my_index, 0, keepdims=False)
    mine_pos = lax.dynamic_index_in_dim(position, my_index, 0, keepdims=False)
    slot_ids = jnp.arange(capacity, dtype=jnp.int32)
    asked = (owners == my_index)[:, :, None] & (position[:, :, None] == slot_ids[None, None, :])
    wanted = jnp.sum(asked.astype(jnp.int32) * within[:, :, None], axis=1)
    pick_back = mine_owner * capacity + mine_pos

    def own_pair(blocks):
        return block_pair(blocks[0], blocks[1], blocks[2], score_scale)

    own_out, own_max, own_sum = lax.map(own_pair, (q_blocks, k_blocks, v_blocks))
    owner_ids = jnp.arange(ctx_count, dtype=jnp.int32)
    chosen = (mine_owner[:, None, None] == owner_ids[None, :, None]) & (
        mine_pos[:, None, None] == slot_ids[None, None, :]
    )
    query_of_slot = jnp.arange(slots, dtype=jnp.int32) // RSEL
    source_block = jnp.sum(chosen.astype(jnp.int32) * query_of_slot[:, None, None], axis=0)
    send_queries = q_blocks[source_block]
    arrived = lax.all_to_all(send_queries, "ctx", split_axis=0, concat_axis=0, tiled=True)
    arrived_flat = arrived.reshape(ctx_count * capacity, BLOCK, heads_here, HD)

    def owner_pair(items):
        query_block, block_index = items
        return block_pair(query_block, k_blocks[block_index], v_blocks[block_index], score_scale)

    remote_out, remote_max, remote_sum = lax.map(owner_pair, (arrived_flat, wanted.reshape(-1)))
    remote_out = remote_out.reshape(ctx_count, capacity, BLOCK, heads_here, HD)
    remote_max = remote_max.reshape(ctx_count, capacity, heads_here, BLOCK)
    remote_sum = remote_sum.reshape(ctx_count, capacity, heads_here, BLOCK)
    back_out, back_max, back_sum = (
        lax.all_to_all(remote_out, "ctx", split_axis=0, concat_axis=0, tiled=True),
        lax.all_to_all(remote_max, "ctx", split_axis=0, concat_axis=0, tiled=True),
        lax.all_to_all(remote_sum, "ctx", split_axis=0, concat_axis=0, tiled=True),
    )
    far_out = back_out.reshape(ctx_count * capacity, BLOCK, heads_here, HD)[pick_back]
    far_max = back_max.reshape(ctx_count * capacity, heads_here, BLOCK)[pick_back]
    far_sum = back_sum.reshape(ctx_count * capacity, heads_here, BLOCK)[pick_back]
    far_out = far_out.reshape(local_blocks, RSEL, BLOCK, heads_here, HD)
    far_max = far_max.reshape(local_blocks, RSEL, heads_here, BLOCK)
    far_sum = far_sum.reshape(local_blocks, RSEL, heads_here, BLOCK)
    overall = jnp.maximum(own_max, jnp.max(far_max, axis=1))
    own_factor = jnp.exp(own_max - overall)
    far_factor = jnp.exp(far_max - overall[:, None])
    numer = own_out * jnp.transpose(own_factor, (0, 2, 1))[..., None]
    numer = numer + jnp.sum(far_out * jnp.transpose(far_factor, (0, 1, 3, 2))[..., None], axis=1)
    denom = own_sum * own_factor + jnp.sum(far_sum * far_factor, axis=1)
    result = (numer / jnp.transpose(denom, (0, 2, 1))[..., None]).astype(jnp.bfloat16)
    result = result.reshape(local_blocks * BLOCK, heads_here, HD)
    restored = lax.all_to_all(result, "head", split_axis=0, concat_axis=1, tiled=True)
    return restored.reshape(tok_rows, HEADS * HD)


def solution(mesh):
    placed = (P(("ctx", "head"), None), P(("ctx", "head"), None), P(("ctx", "head"), None), P())
    return jax.shard_map(
        local, mesh=mesh, in_specs=placed, out_specs=P(("ctx", "head"), None), check_vma=False
    )
```

profile of v0, /device:TPU:164, one launch (start us, length us, event | category | flops | bytes accessed | tf_op | source)
XLA Modules:
  0.0 586.6 jit_solution(18382969166931936499)
XLA Ops:
  0.0 2.4 copy.120
  2.4 5.2 all-to-all-start.1
  8.9 15.3 %all-to-all-done.1 = bf16[256,16,128]{0,2,1:T(8,128)(2,1)S(1)} async-done(((bf16[256,16,128]{0,2,1:T(8,128)(2,1)}), bf16[256,16,128]{0,2,1:T(8,128)(2,1)S(1)}, u32[]{:S(2)}, u32[]{:S(2)}) %all-to-all-start.1) | async-done | bytes 1048608 | tf_op jit(solution)/shard_map/all_to_all | solution.py:50
  24.2 3.7 all-to-all-start
  28.2 2.3 copy.122
  31.1 13.3 %all-to-all-done = bf16[256,16,128]{0,2,1:T(8,128)(2,1)S(1)} async-done(((bf16[256,16,128]{0,2,1:T(8,128)(2,1)}), bf16[256,16,128]{0,2,1:T(8,128)(2,1)S(1)}, u32[]{:S(2)}, u32[]{:S(2)}) %all-to-all-start) | async-done | bytes 1048608 | tf_op jit(solution)/shard_map/all_to_all | solution.py:52
  44.4 4.3 all-to-all-start.2
  49.8 3.1 gather_fusion
  52.9 12.5 %all-to-all-done.2 = bf16[256,16,128]{0,2,1:T(8,128)(2,1)} async-done(((bf16[256,16,128]{0,2,1:T(8,128)(2,1)}), bf16[256,16,128]{0,2,1:T(8,128)(2,1)}, u32[]{:S(2)}, u32[]{:S(2)}) %all-to-all-start.2) | async-done | bytes 1048608 | tf_op jit(solution)/shard_map/all_to_all | solution.py:51
  65.4 9.2 %all-to-all-start.3 = ((bf16[16,2,512,1,128]{4,2,1,3,0:T(8,128)(2,1)}), bf16[16,2,512,1,128]{4,2,1,3,0:T(8,128)(2,1)}, u32[]{:S(2)}, u32[]{:S(2)}) async-start(bf16[16,2,512,1,128]{4,2,1,3,0:T(8,128)(2,1)} %bitcast.142), calls=%async_computation.3 | async-start | bytes 8388608 | tf_op jit(solution)/shard_map/all_to_all | solution.py:79
  75.8 1.6 copy.123
  77.4 89.8 %all-to-all-done.3 = bf16[16,2,512,1,128]{4,2,1,3,0:T(8,128)(2,1)} async-done(((bf16[16,2,512,1,128]{4,2,1,3,0:T(8,128)(2,1)}), bf16[16,2,512,1,128]{4,2,1,3,0:T(8,128)(2,1)}, u32[]{:S(2)}, u32[]{:S(2)}) %all-to-all-start.3) | async-done | bytes 4194336 | tf_op jit(solution)/shard_map/all_to_all | solution.py:79
  167.2 152.0 %while.29 = (s32[]{:T(128)}, f32[32,512,1,128]{1,3,2,0:T(8,128)}, f32[32,1,512]{2,1,0:T(1,128)S(1)}, f32[32,1,512]{2,1,0:T(1,128)S(1)}, s32[32]{0:T(128)S(1)}, /...) while((s32[]{:T(128)}, f32[32,512,1,128]{1,3,2,0:T(8,128)}, ...), condition=%wide.region_11.12_spmd, body=%wide.region_8.11_spmd.sunk | while | flops 135789568 | bytes 3818663 | solution.py:86
  320.0 10.7 %all-to-all-start.4 = ((f32[16,2,1,512]{3,1,2,0:T(2,128)}), f32[16,2,1,512]{3,1,2,0:T(2,128)S(1)}, u32[]{:S(2)}, u32[]{:S(2)}) async-start(f32[16,2,1,512]{3,1,2,0:T(2,128)} %reshape.320), calls=%async_computation.4 | async-start | bytes 131072 | tf_op jit(solution)/shard_map/all_to_all | solution.py:92
  330.9 3.6 all-to-all-done.4
  334.5 12.6 %all_to_all.80 = f32[16,2,1,512]{3,1,2,0:T(2,128)S(1)} all-to-all(f32[16,2,1,512]{3,1,2,0:T(2,128)S(1)} %reshape.326), channel_id=1, replica_groups=mesh['head'=16,'ctx'=16] {'ctx'}, dimensions={0} | all-to-all | bytes 131072 | tf_op jit(solution)/shard_map/all_to_all | solution.py:93
  347.1 10.9 %all-to-all-start.5 = ((f32[16,2,512,1,128]{2,4,1,3,0:T(8,128)}), f32[16,2,512,1,128]{2,4,1,3,0:T(8,128)}, u32[]{:S(2)}, u32[]{:S(2)}) async-start(f32[16,2,512,1,128]{2,4,1,3,0:T(8,128)} %bitcast.144), calls=%async_computation.5 | async-start | bytes 16777216 | tf_op jit(solution)/shard_map/all_to_all | solution.py:91
  358.0 12.5 %while.28 = (s32[]{:T(128)}, f32[8,512,1,128]{1,3,2,0:T(8,128)}, f32[8,1,512]{2,1,0:T(1,128)S(1)}, f32[8,1,512]{2,1,0:T(1,128)S(1)}, bf16[8,512,1,128]{3,1,2,0:T...) while((s32[]{:T(128)}, f32[8,512,1,128]{1,3,2,0:T(8,128)}, ...), condition=%wide.region_3.4_spmd, body=%wide.region_0.3_spmd.sunk | while | flops 135789568 | bytes 3819609 | solution.py:71
  372.1 176.6 %all-to-all-done.5 = f32[16,2,512,1,128]{2,4,1,3,0:T(8,128)} async-done(((f32[16,2,512,1,128]{2,4,1,3,0:T(8,128)}), f32[16,2,512,1,128]{2,4,1,3,0:T(8,128)}, u32[]{:S(2)}, u32[]{:S(2)}) %all-to-all-start.5) | async-done | bytes 8388640 | tf_op jit(solution)/shard_map/all_to_all | solution.py:91
  548.7 6.2 %gather_fusion.2 = f32[16,512,128]{1,2,0:T(8,128)} fusion(f32[32,512,128]{1,2,0:T(8,128)} %bitcast.44, s32[1024]{0:T(1024)S(1)} %pad_clamp_fusion), kind=kCustom, calls=%fused_computation.2 | custom fusion | bytes 8388672 | tf_op jit(solution)/shard_map/gather | solution.py:95
  554.9 3.1 multiply_reduce_fusion
  559.8 1.4 reduce.19
  561.5 21.9 %all_to_all.81 = bf16[16,2,16384]{2,1,0:T(2,128)(2,1)S(1)} all-to-all(bf16[16,2,16384]{2,1,0:T(2,128)(2,1)S(1)} %reshape.387), channel_id=1, replica_groups=mesh['head'=16,'ctx'=16] {'head'}, dimensions={0} | all-to-all | bytes 2097152 | tf_op jit(solution)/shard_map/all_to_all | solution.py:109
  585.1 1.4 copy.143
  (256 shorter events, 120.7 us)
Async XLA Ops:
  0.0 7.6 %copy-start.1 = (bf16[256,2048]{1,0:T(8,128)(2,1)S(1)}, bf16[256,2048]{1,0:T(8,128)(2,1)}, u32[]{:S(2)}) copy-start(bf16[256,2048]{1,0:T(8,128)(2,1)} %param.10) | copy-start | bytes 3145732
  0.0 27.9 %copy-start.2 = (s32[128,2]{0,1:T(2,128)S(1)}, s32[128,2]{0,1:T(2,128)}, u32[]{:S(2)}) copy-start(s32[128,2]{0,1:T(2,128)} %param.11) | copy-start | bytes 3076
  2.4 21.8 %all-to-all-start.1 = ((bf16[256,16,128]{0,2,1:T(8,128)(2,1)}), bf16[256,16,128]{0,2,1:T(8,128)(2,1)S(1)}, u32[]{:S(2)}, u32[]{:S(2)}) async-start(bf16[256,16,128]{0,2,1:T(8,128)(2,1)} %bitcast.22), calls=%async_computation.1 | async-start | bytes 2097152 | tf_op jit(solution)/shard_map/all_to_all | solution.py:50
  24.2 20.2 %all-to-all-start = ((bf16[256,16,128]{0,2,1:T(8,128)(2,1)}), bf16[256,16,128]{0,2,1:T(8,128)(2,1)S(1)}, u32[]{:S(2)}, u32[]{:S(2)}) async-start(bf16[256,16,128]{0,2,1:T(8,128)(2,1)} %bitcast.17), calls=%async_computation | async-start | bytes 2097152 | tf_op jit(solution)/shard_map/all_to_all | solution.py:52
  44.4 21.0 %all-to-all-start.2 = ((bf16[256,16,128]{0,2,1:T(8,128)(2,1)}), bf16[256,16,128]{0,2,1:T(8,128)(2,1)}, u32[]{:S(2)}, u32[]{:S(2)}) async-start(bf16[256,16,128]{0,2,1:T(8,128)(2,1)} %bitcast.27), calls=%async_computation.2 | async-start | bytes 2097152 | tf_op jit(solution)/shard_map/all_to_all | solution.py:51
  65.4 101.9 %all-to-all-start.3 = ((bf16[16,2,512,1,128]{4,2,1,3,0:T(8,128)(2,1)}), bf16[16,2,512,1,128]{4,2,1,3,0:T(8,128)(2,1)}, u32[]{:S(2)}, u32[]{:S(2)}) async-start(bf16[16,2,512,1,128]{4,2,1,3,0:T(8,128)(2,1)} %bitcast.142), calls=%async_computation.3 | async-start | bytes 8388608 | tf_op jit(solution)/shard_map/all_to_all | solution.py:79
  320.0 14.5 %all-to-all-start.4 = ((f32[16,2,1,512]{3,1,2,0:T(2,128)}), f32[16,2,1,512]{3,1,2,0:T(2,128)S(1)}, u32[]{:S(2)}, u32[]{:S(2)}) async-start(f32[16,2,1,512]{3,1,2,0:T(2,128)} %reshape.320), calls=%async_computation.4 | async-start | bytes 131072 | tf_op jit(solution)/shard_map/all_to_all | solution.py:92
  347.1 201.6 %all-to-all-start.5 = ((f32[16,2,512,1,128]{2,4,1,3,0:T(8,128)}), f32[16,2,512,1,128]{2,4,1,3,0:T(8,128)}, u32[]{:S(2)}, u32[]{:S(2)}) async-start(f32[16,2,512,1,128]{2,4,1,3,0:T(8,128)} %bitcast.144), calls=%async_computation.5 | async-start | bytes 16777216 | tf_op jit(solution)/shard_map/all_to_all | solution.py:91
  554.9 3.2 copy-start
where the time goes:
time: 589 us; the launch traced here: 587 us
  waiting for transfers between devices  311 us (53%)
  matrix products  83 us (14%)
  loops' own time  54.6 us (9%)
  local copies, waits for them, and re-layouts  44.7 us (8%)
  starting transfers between devices  43.9 us (7%)
  blocking collectives  34.4 us (6%)
  other arithmetic  14.5 us (2%)
    all_to_all x1, waiting for transfers between devices, local(): lax.all_to_all(remote_out, 'ctx', split_axis=0, concat_axis=0, tiled=True)  177 us
    all_to_all x1, waiting for transfers between devices, local(): lax.all_to_all(send_queries, 'ctx', split_axis=0, concat_axis=0, tiled=True)  89.8 us
    another operation x1, loops' own time, local(): lax.map(owner_pair, (arrived_flat, wanted.reshape(-1)))  54.5 us
    dot_general x40, matrix products, block_pair(): jnp.einsum('qhd,khd->hqk', query_block, key_block, preferred_element_type...  41.5 us
    dot_general x40, matrix products, block_pair(): jnp.einsum('hqk,khd->qhd', weights, value_block, preferred_element_type=j...  41.5 us
    all_to_all x1, blocking collectives, local(): lax.all_to_all(result, 'head', split_axis=0, concat_axis=1, tiled=True)  21.9 us
    dynamic_slice x32, local copies, waits for them, and re-layouts, local(): lax.map(owner_pair, (arrived_flat, wanted.reshape(-1)))  18.6 us
    all_to_all x1, waiting for transfers between devices, local(): lax.all_to_all(q_split, 'head', split_axis=1, concat_axis=0, tiled=True)  15.3 us
  transfers between devices with their start and end apart: 6, of which 6 were waited for; matrix products, arithmetic and copies ran while one was open for 4% of the time, Pallas kernels for 0%

commit v1 on v0

--- a/solution.py
+++ b/solution.py
@@ -49,7 +49,12 @@
     q_heads, k_heads, v_heads = (
         lax.all_to_all(q_split, "head", split_axis=1, concat_axis=0, tiled=True),
         lax.all_to_all(k_split, "head", split_axis=1, concat_axis=0, tiled=True),
-        lax.all_to_all(v_split, "head", split_axis=1, concat_axis=0, tiled=True),
+        jnp.concatenate(
+            lax.all_to_all(
+                jnp.stack(jnp.split(v_split, lax.axis_size("head"), axis=1)), "head", 0, 0
+            ),
+            axis=0,
+        ),
     )
     local_blocks = q_heads.shape[0] // BLOCK
     q_blocks = q_heads.reshape(local_blocks, BLOCK, heads_here, HD)

time: 589 us -> 606 us (1.029)
  local copies, waits for them, and re-layouts: 44.7 us -> 53.3 us
  loops' own time: 54.6 us -> 62.7 us
    another operation x1, loops' own time: 54.5 us -> 62.7 us  [local(): lax.map(owner_pair, (arrived_flat, wanted.reshape(-1)))]
    unnamed x14 -> x33, local copies, waits for them, and re-layouts: 7.43 us -> 15.2 us
where the time goes in v1:
time: 606 us; the launch traced here: 603 us
  waiting for transfers between devices  312 us (51%)
  matrix products  83 us (14%)
  loops' own time  62.7 us (10%)
  local copies, waits for them, and re-layouts  53.3 us (9%)
  starting transfers between devices  43.2 us (7%)
  blocking collectives  34.4 us (6%)
  other arithmetic  14.5 us (2%)
    all_to_all x1, waiting for transfers between devices, local(): lax.all_to_all(remote_out, 'ctx', split_axis=0, concat_axis=0, tiled=True)  177 us
    all_to_all x1, waiting for transfers between devices, local(): lax.all_to_all(send_queries, 'ctx', split_axis=0, concat_axis=0, tiled=True)  89.8 us
    another operation x1, loops' own time, local(): lax.map(owner_pair, (arrived_flat, wanted.reshape(-1)))  62.7 us
    dot_general x40, matrix products, block_pair(): jnp.einsum('qhd,khd->hqk', query_block, key_block, preferred_element_type...  41.5 us
    dot_general x40, matrix products, block_pair(): jnp.einsum('hqk,khd->qhd', weights, value_block, preferred_element_type=j...  41.5 us
    all_to_all x1, blocking collectives, local(): lax.all_to_all(result, 'head', split_axis=0, concat_axis=1, tiled=True)  21.9 us
    dynamic_slice x32, local copies, waits for them, and re-layouts, local(): lax.map(owner_pair, (arrived_flat, wanted.reshape(-1)))  18.8 us
    all_to_all x1, waiting for transfers between devices, local(): lax.all_to_all(jnp.stack(jnp.split(v_split, lax.axis_size('head'), axis=1...  15.3 us
  transfers between devices with their start and end apart: 6, of which 6 were waited for; matrix products, arithmetic and copies ran while one was open for 4% of the time, Pallas kernels for 0%

profile of v1, /device:TPU:164, one launch (start us, length us, event | category | flops | bytes accessed | tf_op | source)
XLA Modules:
  0.0 603.5 jit_solution(2851045664009216031)
XLA Ops:
  0.0 1.6 copy.148
  11.7 5.2 all-to-all-start
  18.3 15.3 %all-to-all-done = bf16[16,256,1,128]{1,3,2,0:T(8,128)(2,1)S(1)} async-done(((bf16[16,256,1,128]{1,3,2,0:T(8,128)(2,1)}), bf16[16,256,1,128]{1,3,2,0:T(8,128)(2,1)S(1)}, u32[]{:S(2)}, u32[]{:S(2)}) %all-to-all-start) | async-done | bytes 1048608 | tf_op jit(solution)/shard_map/all_to_all | solution.py:53
  33.6 3.7 all-to-all-start.1
  37.5 1.3 copy.152
  39.5 14.2 %all-to-all-done.1 = bf16[256,16,128]{0,2,1:T(8,128)(2,1)S(1)} async-done(((bf16[256,16,128]{0,2,1:T(8,128)(2,1)}), bf16[256,16,128]{0,2,1:T(8,128)(2,1)S(1)}, u32[]{:S(2)}, u32[]{:S(2)}) %all-to-all-start.1) | async-done | bytes 1048608 | tf_op jit(solution)/shard_map/all_to_all | solution.py:50
  53.8 3.7 all-to-all-start.2
  58.5 3.1 gather_fusion
  61.6 12.4 %all-to-all-done.2 = bf16[256,16,128]{0,2,1:T(8,128)(2,1)S(1)} async-done(((bf16[256,16,128]{0,2,1:T(8,128)(2,1)}), bf16[256,16,128]{0,2,1:T(8,128)(2,1)S(1)}, u32[]{:S(2)}, u32[]{:S(2)}) %all-to-all-start.2) | async-done | bytes 1048608 | tf_op jit(solution)/shard_map/all_to_all | solution.py:51
  74.0 9.2 %all-to-all-start.3 = ((bf16[16,2,512,1,128]{4,2,1,3,0:T(8,128)(2,1)}), bf16[16,2,512,1,128]{4,2,1,3,0:T(8,128)(2,1)}, u32[]{:S(2)}, u32[]{:S(2)}) async-start(bf16[16,2,512,1,128]{4,2,1,3,0:T(8,128)(2,1)} %bitcast.203), calls=%async_computation.3 | async-start | bytes 8388608 | tf_op jit(solution)/shard_map/all_to_all | solution.py:84
  84.4 1.6 copy.149
  86.1 89.8 %all-to-all-done.3 = bf16[16,2,512,1,128]{4,2,1,3,0:T(8,128)(2,1)} async-done(((bf16[16,2,512,1,128]{4,2,1,3,0:T(8,128)(2,1)}), bf16[16,2,512,1,128]{4,2,1,3,0:T(8,128)(2,1)}, u32[]{:S(2)}, u32[]{:S(2)}) %all-to-all-start.3) | async-done | bytes 4194336 | tf_op jit(solution)/shard_map/all_to_all | solution.py:84
  175.9 160.3 %while.29 = (s32[]{:T(128)}, f32[32,512,1,128]{1,3,2,0:T(8,128)}, f32[32,1,512]{2,1,0:T(1,128)S(1)}, f32[32,1,512]{2,1,0:T(1,128)S(1)}, s32[32]{0:T(128)S(1)}, /...) while((s32[]{:T(128)}, f32[32,512,1,128]{1,3,2,0:T(8,128)}, ...), condition=%wide.region_11.12_spmd, body=%wide.region_8.11_spmd.sunk | while | flops 135789568 | bytes 3818663 | solution.py:91
  337.0 10.6 %all-to-all-start.4 = ((f32[16,2,1,512]{3,1,2,0:T(2,128)}), f32[16,2,1,512]{3,1,2,0:T(2,128)S(1)}, u32[]{:S(2)}, u32[]{:S(2)}) async-start(f32[16,2,1,512]{3,1,2,0:T(2,128)} %reshape.315), calls=%async_computation.4 | async-start | bytes 131072 | tf_op jit(solution)/shard_map/all_to_all | solution.py:97
  347.8 3.6 all-to-all-done.4
  351.4 12.6 %all_to_all.70 = f32[16,2,1,512]{3,1,2,0:T(2,128)S(1)} all-to-all(f32[16,2,1,512]{3,1,2,0:T(2,128)S(1)} %reshape.321), channel_id=1, replica_groups=mesh['head'=16,'ctx'=16] {'ctx'}, dimensions={0} | all-to-all | bytes 131072 | tf_op jit(solution)/shard_map/all_to_all | solution.py:98
  364.0 10.9 %all-to-all-start.5 = ((f32[16,2,512,1,128]{2,4,1,3,0:T(8,128)}), f32[16,2,512,1,128]{2,4,1,3,0:T(8,128)}, u32[]{:S(2)}, u32[]{:S(2)}) async-start(f32[16,2,512,1,128]{2,4,1,3,0:T(8,128)} %bitcast.205), calls=%async_computation.5 | async-start | bytes 16777216 | tf_op jit(solution)/shard_map/all_to_all | solution.py:96
  374.9 12.5 %while.28 = (s32[]{:T(128)}, f32[8,512,1,128]{1,3,2,0:T(8,128)}, f32[8,1,512]{2,1,0:T(1,128)S(1)}, f32[8,1,512]{2,1,0:T(1,128)S(1)}, bf16[8,512,1,128]{3,1,2,0:T...) while((s32[]{:T(128)}, f32[8,512,1,128]{1,3,2,0:T(8,128)}, ...), condition=%wide.region_3.4_spmd, body=%wide.region_0.3_spmd.sunk | while | flops 135789568 | bytes 3819609 | solution.py:76
  389.0 176.6 %all-to-all-done.5 = f32[16,2,512,1,128]{2,4,1,3,0:T(8,128)} async-done(((f32[16,2,512,1,128]{2,4,1,3,0:T(8,128)}), f32[16,2,512,1,128]{2,4,1,3,0:T(8,128)}, u32[]{:S(2)}, u32[]{:S(2)}) %all-to-all-start.5) | async-done | bytes 8388640 | tf_op jit(solution)/shard_map/all_to_all | solution.py:96
  565.6 6.2 %gather_fusion.2 = f32[16,512,128]{1,2,0:T(8,128)} fusion(f32[32,512,128]{1,2,0:T(8,128)} %bitcast.58, s32[1024]{0:T(1024)S(1)} %pad_clamp_fusion), kind=kCustom, calls=%fused_computation.2 | custom fusion | bytes 8388672 | tf_op jit(solution)/shard_map/gather | solution.py:100
  571.8 3.1 multiply_reduce_fusion
  576.7 1.4 reduce.19
  578.5 21.9 %all_to_all.71 = bf16[16,2,16384]{2,1,0:T(2,128)(2,1)S(1)} all-to-all(bf16[16,2,16384]{2,1,0:T(2,128)(2,1)S(1)} %reshape.382), channel_id=1, replica_groups=mesh['head'=16,'ctx'=16] {'head'}, dimensions={0} | all-to-all | bytes 2097152 | tf_op jit(solution)/shard_map/all_to_all | solution.py:114
  602.1 1.4 copy.173
  (276 shorter events, 131.0 us)
Async XLA Ops:
  0.0 17.0 %copy-start.2 = (bf16[256,2048]{1,0:T(8,128)(2,1)S(1)}, bf16[256,2048]{1,0:T(8,128)(2,1)}, u32[]{:S(2)}) copy-start(bf16[256,2048]{1,0:T(8,128)(2,1)} %param.8) | copy-start | bytes 3145732
  1.6 35.6 %copy-start.4 = (s32[128,2]{0,1:T(2,128)S(1)}, s32[128,2]{0,1:T(2,128)}, u32[]{:S(2)}) copy-start(s32[128,2]{0,1:T(2,128)} %param.11) | copy-start | bytes 3076
  2.2 35.3 %copy-start.3 = (bf16[256,2048]{1,0:T(8,128)(2,1)S(1)}, bf16[256,2048]{1,0:T(8,128)(2,1)}, u32[]{:S(2)}) copy-start(bf16[256,2048]{1,0:T(8,128)(2,1)} %param.9) | copy-start | bytes 3145732
  11.7 21.8 %all-to-all-start = ((bf16[16,256,1,128]{1,3,2,0:T(8,128)(2,1)}), bf16[16,256,1,128]{1,3,2,0:T(8,128)(2,1)S(1)}, u32[]{:S(2)}, u32[]{:S(2)}) async-start(bf16[16,256,1,128]{1,3,2,0:T(8,128)(2,1)} %fusion.29), calls=%async_computation | async-start | bytes 2097152 | tf_op jit(solution)/shard_map/all_to_all | solution.py:53
  33.6 24.3 %copy-start = (bf16[16,256,1,128]{1,3,2,0:T(8,128)(2,1)}, bf16[16,256,1,128]{1,3,2,0:T(8,128)(2,1)S(1)}, u32[]{:S(2)}) copy-start(bf16[16,256,1,128]{1,3,2,0:T(8,128)(2,1)S(1)} %all-to-all-done) | copy-start | bytes 3145732
  33.6 20.2 %all-to-all-start.1 = ((bf16[256,16,128]{0,2,1:T(8,128)(2,1)}), bf16[256,16,128]{0,2,1:T(8,128)(2,1)S(1)}, u32[]{:S(2)}, u32[]{:S(2)}) async-start(bf16[256,16,128]{0,2,1:T(8,128)(2,1)} %bitcast.36), calls=%async_computation.1 | async-start | bytes 2097152 | tf_op jit(solution)/shard_map/all_to_all | solution.py:50
  53.8 20.2 %all-to-all-start.2 = ((bf16[256,16,128]{0,2,1:T(8,128)(2,1)}), bf16[256,16,128]{0,2,1:T(8,128)(2,1)S(1)}, u32[]{:S(2)}, u32[]{:S(2)}) async-start(bf16[256,16,128]{0,2,1:T(8,128)(2,1)} %bitcast.228), calls=%async_computation.2 | async-start | bytes 2097152 | tf_op jit(solution)/shard_map/all_to_all | solution.py:51
  74.0 101.9 %all-to-all-start.3 = ((bf16[16,2,512,1,128]{4,2,1,3,0:T(8,128)(2,1)}), bf16[16,2,512,1,128]{4,2,1,3,0:T(8,128)(2,1)}, u32[]{:S(2)}, u32[]{:S(2)}) async-start(bf16[16,2,512,1,128]{4,2,1,3,0:T(8,128)(2,1)} %bitcast.203), calls=%async_computation.3 | async-start | bytes 8388608 | tf_op jit(solution)/shard_map/all_to_all | solution.py:84
  337.0 14.5 %all-to-all-start.4 = ((f32[16,2,1,512]{3,1,2,0:T(2,128)}), f32[16,2,1,512]{3,1,2,0:T(2,128)S(1)}, u32[]{:S(2)}, u32[]{:S(2)}) async-start(f32[16,2,1,512]{3,1,2,0:T(2,128)} %reshape.315), calls=%async_computation.4 | async-start | bytes 131072 | tf_op jit(solution)/shard_map/all_to_all | solution.py:97
  364.0 201.6 %all-to-all-start.5 = ((f32[16,2,512,1,128]{2,4,1,3,0:T(8,128)}), f32[16,2,512,1,128]{2,4,1,3,0:T(8,128)}, u32[]{:S(2)}, u32[]{:S(2)}) async-start(f32[16,2,512,1,128]{2,4,1,3,0:T(8,128)} %bitcast.205), calls=%async_computation.5 | async-start | bytes 16777216 | tf_op jit(solution)/shard_map/all_to_all | solution.py:96
  571.8 3.2 copy-start.1
